TPU v7x, 32 devices: a whole 2x2x4 slice. The times are simulated.
32 devices in a mesh: dom: 4 (over z), blk: 8 (over y, x, core).
Axes of the slice: x: 2, y: 2, z: 4, core: 2. Of those that a mesh axis runs over, the one named last changes fastest.
Arguments:
- features: bfloat16 [16384, 128], P(('dom', 'blk')), may hold values from -6 to 6
- history: bfloat16 [16384, 512], P(('dom', 'blk')), may hold values from 0 to 1.5
- adj_tiles: bfloat16 [16384, 4, 512], P(('dom', 'blk')), may hold values from -0.109375 to 0.109375
- tile_cols: int32 [4, 8, 4], P('dom', 'blk'), may hold values from 0 to 7, as said below
- bound_one: bfloat16 [16384, 1024], P(('dom', 'blk')), may hold values from -0.109375 to 0.109375
- bound_two: bfloat16 [16384, 1024], P(('dom', 'blk')), may hold values from -0.109375 to 0.109375
- block_ids: int32 [2, 4, 8, 4, 2], P(None, 'dom', 'blk'), may hold values from 0 to 3
- block_counts: int32 [2, 4, 8, 4], P(None, 'dom', 'blk'), may hold values from 0 to 2, as said below
- w_in: bfloat16 [128, 512], replicated, may hold values from -0.5 to 0.5
- b_in: float32 [512], replicated, may hold values from -3 to 3
- w_out: bfloat16 [512, 512], replicated, may hold values from -0.25 to 0.25
- b_out: float32 [512], replicated, may hold values from -3 to 3
Outputs:
- fresh_history: bfloat16 [16384, 512], P(('dom', 'blk'))
- node_out: bfloat16 [16384, 512], P(('dom', 'blk'))
Inputs may be any that keep to these rules, and one draw needn't show every extreme that they name: `tile_cols`: each device's list names 4 distinct blk indices, its own first. `block_counts`: zero where owner and reader are the same partition; for every layer and reader partition some blk index receives 2 live slots from every other partition.
All inputs are finite; a program needn't handle non-finite values.
Results may differ from a plain program's by a relative error of at most 0.0055.
Values may be sent and summed in bfloat16 or wider, within the bound.
No kernel may reach another device: no remote copies, remote signals or barrier semaphores. Data moves between devices by JAX's collectives and lax.ppermute only.
A program may use at most 64 MiB of HBM per device.

v0:
```python
import functools

import jax
import jax.numpy as jnp
from jax import lax
from jax.experimental import pallas as pl
from jax.experimental.pallas import tpu as pltpu
from jax.sharding import PartitionSpec as P


BF16 = jnp.bfloat16
F32 = jnp.float32
VMEM = pl.BlockSpec(memory_space=pltpu.VMEM)
MIB = 1 << 20
SMEM = pl.BlockSpec(memory_space=pltpu.SMEM)


def far(array):
    return pltpu.with_memory_space_constraint(array, pltpu.HBM)


def near(array):
    return pltpu.with_memory_space_constraint(array, pltpu.VMEM)


def dot(a, b):
    return jnp.dot(a, b, preferred_element_type=F32)


def pack_kernel(*refs):
    layers, slots, n_dom = refs[0].shape[0], *refs[0].shape[-2:]
    came_refs = refs[:layers + 2]
    out_refs = refs[layers + 3:-layers - 2]
    *held_refs, sems = refs[-layers - 2:]
    held_refs.insert(2, refs[layers + 2])
    ids_ref, counts_ref, *panel_refs = held_refs
    copies = [pltpu.make_async_copy(*pair, sems.at[n]) for n, pair in enumerate(zip(came_refs, held_refs))]
    for copy in copies:
        copy.start()
    copies[0].wait()
    copies[1].wait()
    dom = lax.axis_index("dom")
    for layer in range(layers):
        copies[2 + layer].wait()
        for apart in range(1, n_dom):
            out_ref = out_refs[layer * (n_dom - 1) + apart - 1]
            rows, width = out_ref.shape[0] // slots, out_ref.shape[1]
            reader = lax.bitwise_xor(dom, apart)
            live = counts_ref[layer, 0, 0, reader]
            for slot in range(slots):
                start = pl.multiple_of(ids_ref[layer, 0, 0, slot, reader] * rows, rows)
                here = pl.ds(slot * rows, rows)

                @pl.when(slot < live)
                def _():
                    out_ref[here, :] = panel_refs[layer][pl.ds(start, rows), :]

                @pl.when(slot >= live)
                def _():
                    out_ref[here, :] = jnp.zeros((rows, width), out_ref.dtype)


def pack(ids, counts, panels, slot_rows):
    n_dom = ids.shape[-1]
    panel, *blocks = pl.pallas_call(
        pack_kernel,
        out_shape=[pltpu.VMEM(panels[0].shape, panels[0].dtype)] + [pltpu.VMEM((slot_rows, panel.shape[1]), panel.dtype) for panel in panels for _ in range(n_dom - 1)],
        in_specs=[pl.BlockSpec(memory_space=pltpu.HBM)] * (2 + len(panels)),
        out_specs=[VMEM] * (1 + len(panels) * (n_dom - 1)),
        scratch_shapes=[pltpu.SMEM(a.shape, a.dtype) for a in (ids, counts)]
        + [pltpu.VMEM(panel.shape, panel.dtype) for panel in panels[1:]]
        + [pltpu.SemaphoreType.DMA((2 + len(panels),))],
        compiler_params=pltpu.CompilerParams(vmem_limit_bytes=2 * MIB),
        name="pack",
    )(*map(far, (ids, counts, *panels)))
    return panel, *(blocks[n * (n_dom - 1):(n + 1) * (n_dom - 1)] for n in range(len(panels)))


def stack_panels(panel_refs, stack_ref):
    rows = panel_refs[0].shape[0]
    for at, panel_ref in enumerate(panel_refs):
        stack_ref[at * rows:(at + 1) * rows, :] = panel_ref[...]


def tile_rows(cols_ref, k, rows):
    apart = lax.bitwise_xor(cols_ref[0, 0, k], lax.axis_index("blk"))
    return pl.ds(pl.multiple_of(apart * rows, rows), rows)


def border_product(dom, bound_ref, border_refs, distances):
    total = None
    for border_ref, apart in zip(border_refs, distances):
        width = border_ref.shape[0]
        owner = lax.bitwise_xor(dom, apart)
        part = dot(bound_ref[:, pl.ds(pl.multiple_of(owner * width, width), width)], border_ref[...])
        total = part if total is None else total + part
    return total


def early_kernel(adj_ref, panel_ref, tiles_ref, total_ref, held_ref, sems):
    rows = panel_ref.shape[0]
    chunks = sems.shape[0]
    step = rows // chunks
    parts = [pl.ds(n * step, step) for n in range(chunks)]
    copies = [pltpu.make_async_copy(adj_ref.at[here], held_ref.at[here], sems.at[n]) for n, here in enumerate(parts)]
    for copy in copies:
        copy.start()
    for copy, here in zip(copies, parts):
        copy.wait()
        tiles_ref[here, :] = held_ref[here].reshape(step, tiles_ref.shape[1])
    total_ref[...] = dot(tiles_ref[:, :rows], panel_ref[...])


def early_part(adj, panel):
    return pl.pallas_call(
        early_kernel,
        out_shape=[pltpu.VMEM((adj.shape[0], adj.shape[1] * adj.shape[2]), BF16), pltpu.VMEM(panel.shape, F32)],
        in_specs=[pl.BlockSpec(memory_space=pltpu.HBM), VMEM],
        out_specs=[VMEM] * 2,
        scratch_shapes=[pltpu.VMEM(adj.shape, BF16), pltpu.SemaphoreType.DMA((4,))],
        compiler_params=pltpu.CompilerParams(vmem_limit_bytes=12 * MIB),
        name="early",
    )(far(adj), near(panel))


def first_kernel(n_blk, cols_ref, tiles_ref, total_ref, bound_ref, *refs):
    panel_refs, border_refs, (agg_ref, stack_ref) = refs[:n_blk], refs[n_blk:-2], refs[-2:]
    rows = agg_ref.shape[0]
    stack_panels(panel_refs, stack_ref)
    total = total_ref[...] + border_product(lax.axis_index("dom"), bound_ref, border_refs, range(1, len(border_refs) + 1))
    for k in range(1, cols_ref.shape[-1]):
        total = total + dot(tiles_ref[:, k * rows:(k + 1) * rows], stack_ref[tile_rows(cols_ref, k, rows), :])
    agg_ref[...] = total.astype(BF16)


def first_layer(cols, tiles, total, bound, panels, border):
    shape = panels[0].shape
    return pl.pallas_call(
        functools.partial(first_kernel, len(panels)),
        out_shape=pltpu.VMEM(shape, BF16),
        in_specs=[SMEM] + [VMEM] * (3 + len(panels) + len(border)),
        out_specs=VMEM,
        scratch_shapes=[pltpu.VMEM((len(panels) * shape[0], shape[1]), BF16)],
        compiler_params=pltpu.CompilerParams(vmem_limit_bytes=8 * MIB),
        name="first",
    )(cols, *map(near, (tiles, total, bound, *panels, *border)))


def hidden(agg, w_ref, b_ref):
    return jnp.maximum(dot(agg, w_ref[...]) + b_ref[...], 0.0).astype(BF16)


def own_kernel(distances, tiles_ref, w_ref, b_ref, agg_ref, bound_ref, *refs):
    border_refs, (fresh_ref, total_ref) = refs[:-2], refs[-2:]
    fresh = hidden(agg_ref[...], w_ref, b_ref)
    fresh_ref[...] = fresh
    total = dot(tiles_ref[:, :fresh.shape[0]], fresh)
    if distances:
        total = total + border_product(lax.axis_index("dom"), bound_ref, border_refs, distances)
    total_ref[...] = total


def own_part(tiles, w_in, b_in, agg, bound, border):
    shape = (agg.shape[0], w_in.shape[1])
    return pl.pallas_call(
        functools.partial(own_kernel, tuple(border)),
        out_shape=[jax.ShapeDtypeStruct(shape, BF16), pltpu.VMEM(shape, F32)],
        in_specs=[VMEM] * (5 + len(border)),
        out_specs=[VMEM] * 2,
        compiler_params=pltpu.CompilerParams(vmem_limit_bytes=6 * MIB),
        name="own",
    )(*map(near, (tiles, w_in, b_in, agg, bound, *border.values())))


def others_kernel(n_blk, distances, cols_ref, tiles_ref, w_ref, b_ref, total_ref, bound_ref, *refs):
    panel_refs, border_refs = refs[:n_blk], refs[n_blk:-3]
    sum_ref, stack_ref, fresh_ref = refs[-3:]
    rows = panel_refs[0].shape[0]
    stack_panels(panel_refs, stack_ref)
    for k in range(1, cols_ref.shape[-1]):
        fresh_ref[(k - 1) * rows:k * rows, :] = hidden(stack_ref[tile_rows(cols_ref, k, rows), :], w_ref, b_ref)
    total = total_ref[...] + dot(tiles_ref[:, rows:], fresh_ref[...])
    if distances:
        total = total + border_product(lax.axis_index("dom"), bound_ref, border_refs, distances)
    sum_ref[...] = total


def others_part(cols, tiles, w_in, b_in, total, bound, panels, border):
    rows, width = panels[0].shape
    return pl.pallas_call(
        functools.partial(others_kernel, len(panels), tuple(border)),
        out_shape=pltpu.VMEM(total.shape, F32),
        in_specs=[SMEM] + [VMEM] * (5 + len(panels) + len(border)),
        out_specs=VMEM,
        scratch_shapes=[
            pltpu.VMEM((len(panels) * rows, width), BF16),
            pltpu.VMEM((tiles.shape[1] - rows, total.shape[1]), BF16),
        ],
        compiler_params=pltpu.CompilerParams(vmem_limit_bytes=16 * MIB),
        name="others",
    )(cols, *map(near, (tiles, w_in, b_in, total, bound, *panels, *border.values())))


def last_kernel(distances, total_ref, bound_ref, w_ref, b_ref, *refs):
    border_refs = refs[:len(distances)]
    out_ref, held_ref, sems = refs[len(distances):]
    dom = lax.axis_index("dom")
    chunks = sems.shape[0]
    rows = total_ref.shape[0] // chunks
    copies = []
    for n in range(chunks):
        here = pl.ds(n * rows, rows)
        total = total_ref[here, :] + border_product(dom, bound_ref.at[here, :], border_refs, distances)
        held_ref[here, :] = (dot(total.astype(BF16), w_ref[...]) + b_ref[...]).astype(BF16)
        copies.append(pltpu.make_async_copy(held_ref.at[here, :], out_ref.at[here, :], sems.at[n]))
        copies[n].start()
    for copy in copies:
        copy.wait()


def last_layer(total, bound, w_out, b_out, border):
    shape = (total.shape[0], w_out.shape[1])
    return pl.pallas_call(
        functools.partial(last_kernel, tuple(border)),
        out_shape=jax.ShapeDtypeStruct(shape, BF16),
        in_specs=[VMEM] * (4 + len(border)),
        out_specs=pl.BlockSpec(memory_space=pltpu.HBM),
        scratch_shapes=[pltpu.VMEM(shape, BF16), pltpu.SemaphoreType.DMA((2,))],
        compiler_params=pltpu.CompilerParams(vmem_limit_bytes=6 * MIB),
        name="last",
    )(*map(near, (total, bound, w_out, b_out, *border.values())))


def swap(block, axis, apart):
    return lax.ppermute(block, axis, [(i, i ^ apart) for i in range(lax.axis_size(axis))])


def all_panels(panel):
    n_blk = lax.axis_size("blk")
    panels = {0: panel}
    far = range(2, n_blk, 2)
    for d in (1, *far):
        panels[d] = swap(panel, "blk", d)
    for d in far:
        panels[d + 1] = swap(panels[d], "blk", 1)
    return [panels[d] for d in range(n_blk)]


def borders(blocks):
    return [swap(block, "dom", apart) for apart, block in enumerate(blocks, 1)]


def body(features, history, adj_tiles, tile_cols, bound_one, bound_two, block_ids, block_counts, w_in, b_in, w_out, b_out):
    slot_rows = bound_one.shape[1] // lax.axis_size("dom")
    ids = block_ids.swapaxes(3, 4)
    b_in, b_out = b_in.reshape(1, -1), b_out.reshape(1, -1)
    features, out_one, out_two = pack(ids, block_counts, (features, history), slot_rows)
    border_one = borders(out_one)
    panels_one = all_panels(features)
    border_two = borders(out_two)
    tiles, total = early_part(adj_tiles, features)
    agg = first_layer(tile_cols, tiles, total, bound_one, panels_one, border_one)
    panels_two = all_panels(agg)
    border_two = dict(enumerate(border_two, 1))
    soon, late = ({d: border_two[d] for d in distances} for distances in soon_and_late(len(border_two) + 1))
    rest = {d: block for d, block in border_two.items() if d not in soon and d not in late}
    fresh, total = own_part(tiles, w_in, b_in, agg, bound_two, soon)
    total = others_part(tile_cols, tiles, w_in, b_in, total, bound_two, panels_two, rest)
    out = last_layer(total, bound_two, w_out, b_out, late)
    return fresh, out


def soon_and_late(n_dom):
    return [], [1, *range(3, n_dom)]


def solution(mesh):
    rows = P(("dom", "blk"), None)
    placed = (
        rows,
        rows,
        P(("dom", "blk"), None, None),
        P("dom", "blk", None),
        rows,
        rows,
        P(None, "dom", "blk", None, None),
        P(None, "dom", "blk", None),
        P(),
        P(),
        P(),
        P(),
    )
    return jax.shard_map(body, mesh=mesh, in_specs=placed, out_specs=(rows, rows), check_vma=False)
```

profile of v0, /device:TPU:0, one launch (start us, length us, event | category | flops | bytes accessed | tf_op | source)
XLA Modules:
  0.0 47.0 jit_solution(12808405662902393997)
XLA Ops:
  0.6 0.0 copy-start.6
  0.6 0.0 copy-start.1
  0.7 1.3 %pack.1 = (bf16[512,128]{1,0:T(8,128)(2,1)S(1)}, bf16[256,128]{1,0:T(8,128)(2,1)S(1)}, bf16[256,128]{1,0:T(8,128)(2,1)S(1)}, bf16[256,128]{1,0:T(8,128)(2,1)S(1)...) custom-call(s32[2,1,1,2,4]{4,3,2,1,0:T(2,128)} %bitcast.6, ...), custom_call_target="tpu_custom_call" | custom-call | tf_op jit(solution)/shard_map/pack/pallas_call | solution.py:65
  2.0 4.0 %collective-permute-start.5 = (bf16[512,128]{1,0:T(8,128)(2,1)S(1)}, bf16[512,128]{1,0:T(8,128)(2,1)S(1)}, u32[]{:S(2)}, u32[]{:S(2)}) collective-permute-start(bf16[512,128]{1,0:T(8,128)(2,1)S(1)} %get-tuple-element.13.panel_ref.refs_0_), channel_id=1, source_target_pairs={{0,6},{1,7},{2,4},{3,5},{4,2},{5,3},{6,0},{7,1},{8,14},{9,15},{10,... | collective-permute-start | bytes 393224 | tf_op jit(solution)/shard_map/ppermute | solution.py:235
  6.0 0.5 %collective-permute-start.3 = (bf16[512,128]{1,0:T(8,128)(2,1)S(1)}, bf16[512,128]{1,0:T(8,128)(2,1)S(1)}, u32[]{:S(2)}, u32[]{:S(2)}) collective-permute-start(bf16[512,128]{1,0:T(8,128)(2,1)S(1)} %get-tuple-element.13.panel_ref.refs_0_), channel_id=1, source_target_pairs={{0,4},{1,5},{2,6},{3,7},{4,0},{5,1},{6,2},{7,3},{8,12},{9,13},{10,... | collective-permute-start | bytes 393224 | tf_op jit(solution)/shard_map/ppermute | solution.py:235
  6.5 0.1 collective-permute-start.1
  6.6 2.0 %collective-permute-start.7 = (bf16[256,128]{1,0:T(8,128)(2,1)S(1)}, bf16[256,128]{1,0:T(8,128)(2,1)S(1)}, u32[]{:S(2)}, u32[]{:S(2)}) collective-permute-start(bf16[256,128]{1,0:T(8,128)(2,1)S(1)} %get-tuple-element.16), channel_id=1, source_target_pairs={{0,8},{8,0},{16,24},{24,16},{1,9},{9,1},{17,25},{25,17},{2,10},{10... | collective-permute-start | bytes 196616 | tf_op jit(solution)/shard_map/ppermute | solution.py:235
  8.6 2.6 %collective-permute-start.8 = (bf16[256,128]{1,0:T(8,128)(2,1)S(1)}, bf16[256,128]{1,0:T(8,128)(2,1)S(1)}, u32[]{:S(2)}, u32[]{:S(2)}) collective-permute-start(bf16[256,128]{1,0:T(8,128)(2,1)S(1)} %get-tuple-element.17), channel_id=1, source_target_pairs={{0,16},{8,24},{16,0},{24,8},{1,17},{9,25},{17,1},{25,9},{2,18},{10... | collective-permute-start | bytes 196616 | tf_op jit(solution)/shard_map/ppermute | solution.py:235
  11.2 0.0 collective-permute-done.7.refs_8_
  11.2 3.7 %collective-permute-start.9 = (bf16[256,128]{1,0:T(8,128)(2,1)S(1)}, bf16[256,128]{1,0:T(8,128)(2,1)S(1)}, u32[]{:S(2)}, u32[]{:S(2)}) collective-permute-start(bf16[256,128]{1,0:T(8,128)(2,1)S(1)} %get-tuple-element.18), channel_id=1, source_target_pairs={{0,24},{8,16},{16,8},{24,0},{1,25},{9,17},{17,9},{25,1},{2,26},{10... | collective-permute-start | bytes 196616 | tf_op jit(solution)/shard_map/ppermute | solution.py:235
  14.9 1.0 %collective-permute-done.8.refs_9_ = bf16[256,128]{1,0:T(8,128)(2,1)S(1)} collective-permute-done((bf16[256,128]{1,0:T(8,128)(2,1)S(1)}, bf16[256,128]{1,0:T(8,128)(2,1)S(1)}, u32[]{:S(2)}, u32[]{:S(2)}) %collective-permute-start.8) | collective-permute-done | bytes 65568 | tf_op jit(solution)/shard_map/ppermute | solution.py:235
  15.8 0.0 collective-permute-start
  15.8 0.0 collective-permute-done.5.refs_6_
  15.8 0.5 %collective-permute-start.6 = (bf16[512,128]{1,0:T(8,128)(2,1)S(1)}, bf16[512,128]{1,0:T(8,128)(2,1)S(1)}, u32[]{:S(2)}, u32[]{:S(2)}) collective-permute-start(bf16[512,128]{1,0:T(8,128)(2,1)S(1)} %collective-permute-done.5.refs_6_), channel_id=1, source_target_pairs={{0,1},{1,0},{2,3},{3,2},{4,5},{5,4},{6,7},{7,6},{8,9},{9,8},{10,11... | collective-permute-start | bytes 393224 | tf_op jit(solution)/shard_map/ppermute | solution.py:235
  16.3 0.0 collective-permute-done.3.refs_4_
  16.3 0.1 collective-permute-start.4
  16.4 0.0 collective-permute-done.1.refs_2_
  16.4 0.4 collective-permute-start.2
  16.9 0.5 %collective-permute-done.9.refs_10_ = bf16[256,128]{1,0:T(8,128)(2,1)S(1)} collective-permute-done((bf16[256,128]{1,0:T(8,128)(2,1)S(1)}, bf16[256,128]{1,0:T(8,128)(2,1)S(1)}, u32[]{:S(2)}, u32[]{:S(2)}) %collective-permute-start.9) | collective-permute-done | bytes 65568 | tf_op jit(solution)/shard_map/ppermute | solution.py:235
  17.3 0.8 %collective-permute-start.17 = (bf16[256,512]{1,0:T(8,128)(2,1)S(1)}, bf16[256,512]{1,0:T(8,128)(2,1)S(1)}, u32[]{:S(2)}, u32[]{:S(2)}) collective-permute-start(bf16[256,512]{1,0:T(8,128)(2,1)S(1)} %get-tuple-element.21), channel_id=1, source_target_pairs={{0,16},{8,24},{16,0},{24,8},{1,17},{9,25},{17,1},{25,9},{2,18},{10... | collective-permute-start | bytes 786440 | tf_op jit(solution)/shard_map/ppermute | solution.py:235
  18.1 1.9 %early.1 = (bf16[512,2048]{1,0:T(8,128)(2,1)S(1)}, f32[512,128]{1,0:T(8,128)S(1)}) custom-call(bf16[512,4,512]{2,1,0:T(4,128)(2,1)} %adj_ref.1, bf16[512,128]{1,0:T(8,128)(2,1)S(1)} %get-tuple-element.13.panel_ref.refs_0_), custom_call_target="tpu_custom_call" | custom-call | tf_op jit(solution)/shard_map/early/pallas_call | solution.py:115
  20.0 0.0 collective-permute-done.refs_1_
  20.0 0.0 collective-permute-done.6.refs_7_
  20.0 0.0 collective-permute-done.4.refs_5_
  20.0 0.0 collective-permute-done.2.refs_3_
  20.0 0.0 copy-done.6
  20.1 0.0 copy-done.1
  20.1 0.0 copy-start
  20.1 0.0 copy-start.3
  20.1 0.0 copy-start.4
  20.1 1.4 %first.1.agg_ref.refs_0_ = bf16[512,128]{1,0:T(8,128)(2,1)S(1)} custom-call(s32[1,1,4]{2,1,0:T(1,128)S(1)} %copy-done.6, bf16[512,2048]{1,0:T(8,128)(2,1)S(1)} %get-tuple-element.14.tiles_ref, f32[512,128]{1,0:T(8,128)S(1)} %get-tuple-element.15.total_ref, bf16[512,1024]{1,0:T(8,128)(2,1)S(1)} %copy-done.1, ...), custom_call_target="tpu_custom_call" | custom-call | tf_op jit(solution)/shard_map/first/pallas_call | solution.py:138
  21.5 2.5 %collective-permute-start.15 = (bf16[512,128]{1,0:T(8,128)(2,1)S(1)}, bf16[512,128]{1,0:T(8,128)(2,1)S(1)}, u32[]{:S(2)}, u32[]{:S(2)}) collective-permute-start(bf16[512,128]{1,0:T(8,128)(2,1)S(1)} %first.1.agg_ref.refs_0_), channel_id=1, source_target_pairs={{0,6},{1,7},{2,4},{3,5},{4,2},{5,3},{6,0},{7,1},{8,14},{9,15},{10,... | collective-permute-start | bytes 393224 | tf_op jit(solution)/shard_map/ppermute | solution.py:235
  24.0 0.5 %collective-permute-start.13 = (bf16[512,128]{1,0:T(8,128)(2,1)S(1)}, bf16[512,128]{1,0:T(8,128)(2,1)S(1)}, u32[]{:S(2)}, u32[]{:S(2)}) collective-permute-start(bf16[512,128]{1,0:T(8,128)(2,1)S(1)} %first.1.agg_ref.refs_0_), channel_id=1, source_target_pairs={{0,4},{1,5},{2,6},{3,7},{4,0},{5,1},{6,2},{7,3},{8,12},{9,13},{10,... | collective-permute-start | bytes 393224 | tf_op jit(solution)/shard_map/ppermute | solution.py:235
  24.5 0.5 %collective-permute-start.11 = (bf16[512,128]{1,0:T(8,128)(2,1)S(1)}, bf16[512,128]{1,0:T(8,128)(2,1)S(1)}, u32[]{:S(2)}, u32[]{:S(2)}) collective-permute-start(bf16[512,128]{1,0:T(8,128)(2,1)S(1)} %first.1.agg_ref.refs_0_), channel_id=1, source_target_pairs={{0,2},{1,3},{2,0},{3,1},{4,6},{5,7},{6,4},{7,5},{8,10},{9,11},{10,... | collective-permute-start | bytes 393224 | tf_op jit(solution)/shard_map/ppermute | solution.py:235
  25.0 0.0 collective-permute-start.10
  25.1 6.4 %collective-permute-done.17.refs_8_ = bf16[256,512]{1,0:T(8,128)(2,1)S(1)} collective-permute-done((bf16[256,512]{1,0:T(8,128)(2,1)S(1)}, bf16[256,512]{1,0:T(8,128)(2,1)S(1)}, u32[]{:S(2)}, u32[]{:S(2)}) %collective-permute-start.17) | collective-permute-done | bytes 262176 | tf_op jit(solution)/shard_map/ppermute | solution.py:235
  31.5 0.0 collective-permute-start.18
  31.5 0.0 collective-permute-done.15.refs_6_
  31.5 1.7 %collective-permute-start.19 = (bf16[256,512]{1,0:T(8,128)(2,1)S(1)}, bf16[256,512]{1,0:T(8,128)(2,1)S(1)}, u32[]{:S(2)}, u32[]{:S(2)}) collective-permute-start(bf16[256,512]{1,0:T(8,128)(2,1)S(1)} %get-tuple-element.23), channel_id=1, source_target_pairs={{0,24},{8,16},{16,8},{24,0},{1,25},{9,17},{17,9},{25,1},{2,26},{10... | collective-permute-start | bytes 786440 | tf_op jit(solution)/shard_map/ppermute | solution.py:235
  33.2 0.0 collective-permute-done.13.refs_4_
  33.2 0.0 collective-permute-start.16
  33.2 0.0 collective-permute-done.11.refs_2_
  33.2 0.5 %collective-permute-start.14 = (bf16[512,128]{1,0:T(8,128)(2,1)S(1)}, bf16[512,128]{1,0:T(8,128)(2,1)S(1)}, u32[]{:S(2)}, u32[]{:S(2)}) collective-permute-start(bf16[512,128]{1,0:T(8,128)(2,1)S(1)} %collective-permute-done.13.refs_4_), channel_id=1, source_target_pairs={{0,1},{1,0},{2,3},{3,2},{4,5},{5,4},{6,7},{7,6},{8,9},{9,8},{10,11... | collective-permute-start | bytes 393224 | tf_op jit(solution)/shard_map/ppermute | solution.py:235
  33.7 0.0 collective-permute-done.10.refs_1_
  33.7 0.1 collective-permute-start.12
  33.8 0.0 copy-done
  33.8 0.0 copy-done.3
  33.8 0.0 copy-done.4
  33.8 1.2 %own.1 = (bf16[512,512]{1,0:T(8,128)(2,1)}, f32[512,512]{1,0:T(8,128)S(1)}) custom-call(bf16[512,2048]{1,0:T(8,128)(2,1)S(1)} %get-tuple-element.14.tiles_ref, bf16[128,512]{1,0:T(8,128)(2,1)S(1)} %copy-done.3, f32[1,512]{1,0:T(1,128)S(1)} %bitcast.3, bf16[512,128]{1,0:T(8,128)(2,1)S(1)} %first.1.agg_ref.refs_0_, bf16[512,1024]{1,0:T(8,128)(2,1)S(1)} %copy-done), custom_call_target="tpu_custom_call" | custom-call | tf_op jit(solution)/shard_map/own/pallas_call | solution.py:165
  35.0 0.0 collective-permute-done.16.refs_7_
  35.0 0.0 collective-permute-done.14.refs_5_
  35.0 0.1 collective-permute-done.12.refs_3_
  35.0 0.0 copy-start.2
  35.0 0.0 copy-start.5
  35.0 2.1 %others.1.total_ref = f32[512,512]{1,0:T(8,128)S(1)} custom-call(s32[1,1,4]{2,1,0:T(1,128)S(1)} %copy-done.6, bf16[512,2048]{1,0:T(8,128)(2,1)S(1)} %get-tuple-element.14.tiles_ref, bf16[128,512]{1,0:T(8,128)(2,1)S(1)} %copy-done.3, f32[1,512]{1,0:T(1,128)S(1)} %bitcast.4, f32[512,512]{1,0:T(8,128)S(1)} %get-tuple-element.20.total_ref, ...), custom_call_target="tpu_custom_call" | custom-call | tf_op jit(solution)/shard_map/others/pallas_call | solution.py:190
  37.2 3.2 %collective-permute-done.18.refs_0_ = bf16[256,512]{1,0:T(8,128)(2,1)S(1)} collective-permute-done((bf16[256,512]{1,0:T(8,128)(2,1)S(1)}, bf16[256,512]{1,0:T(8,128)(2,1)S(1)}, u32[]{:S(2)}, u32[]{:S(2)}) %collective-permute-start.18) | collective-permute-done | bytes 262176 | tf_op jit(solution)/shard_map/ppermute | solution.py:235
  40.4 5.0 %collective-permute-done.19.refs_1_ = bf16[256,512]{1,0:T(8,128)(2,1)S(1)} collective-permute-done((bf16[256,512]{1,0:T(8,128)(2,1)S(1)}, bf16[256,512]{1,0:T(8,128)(2,1)S(1)}, u32[]{:S(2)}, u32[]{:S(2)}) %collective-permute-start.19) | collective-permute-done | bytes 262176 | tf_op jit(solution)/shard_map/ppermute | solution.py:235
  45.4 0.0 copy-done.2
  45.4 0.0 copy-done.5
  45.4 1.6 %last.1 = bf16[512,512]{1,0:T(8,128)(2,1)} custom-call(f32[512,512]{1,0:T(8,128)S(1)} %others.1.total_ref, bf16[512,1024]{1,0:T(8,128)(2,1)S(1)} %copy-done, bf16[512,512]{1,0:T(8,128)(2,1)S(1)} %copy-done.2, f32[1,512]{1,0:T(1,128)S(1)} %bitcast.5, bf16[256,512]{1,0:T(8,128)(2,1)S(1)} %collective-permute-done.18.refs_0_, ...), custom_call_target="tpu_custom_call" | custom-call | tf_op jit(solution)/shard_map/last/pallas_call | solution.py:223
Async XLA Ops:
  0.6 19.4 %copy-start.6 = (s32[1,1,4]{2,1,0:T(1,128)S(1)}, s32[1,1,4]{2,1,0:T(1,128)}, u32[]{:S(2)}) copy-start(s32[1,1,4]{2,1,0:T(1,128)} %cols_ref.3) | copy-start | bytes 52
  0.6 19.4 %copy-start.1 = (bf16[512,1024]{1,0:T(8,128)(2,1)S(1)}, bf16[512,1024]{1,0:T(8,128)(2,1)}, u32[]{:S(2)}) copy-start(bf16[512,1024]{1,0:T(8,128)(2,1)} %bound_ref.4) | copy-start | bytes 3145732
  2.0 13.8 %collective-permute-start.5 = (bf16[512,128]{1,0:T(8,128)(2,1)S(1)}, bf16[512,128]{1,0:T(8,128)(2,1)S(1)}, u32[]{:S(2)}, u32[]{:S(2)}) collective-permute-start(bf16[512,128]{1,0:T(8,128)(2,1)S(1)} %get-tuple-element.13.panel_ref.refs_0_), channel_id=1, source_target_pairs={{0,6},{1,7},{2,4},{3,5},{4,2},{5,3},{6,0},{7,1},{8,14},{9,15},{10,... | collective-permute-start | bytes 393224 | tf_op jit(solution)/shard_map/ppermute | solution.py:235
  6.0 10.4 %collective-permute-start.3 = (bf16[512,128]{1,0:T(8,128)(2,1)S(1)}, bf16[512,128]{1,0:T(8,128)(2,1)S(1)}, u32[]{:S(2)}, u32[]{:S(2)}) collective-permute-start(bf16[512,128]{1,0:T(8,128)(2,1)S(1)} %get-tuple-element.13.panel_ref.refs_0_), channel_id=1, source_target_pairs={{0,4},{1,5},{2,6},{3,7},{4,0},{5,1},{6,2},{7,3},{8,12},{9,13},{10,... | collective-permute-start | bytes 393224 | tf_op jit(solution)/shard_map/ppermute | solution.py:235
  6.5 9.9 %collective-permute-start.1 = (bf16[512,128]{1,0:T(8,128)(2,1)S(1)}, bf16[512,128]{1,0:T(8,128)(2,1)S(1)}, u32[]{:S(2)}, u32[]{:S(2)}) collective-permute-start(bf16[512,128]{1,0:T(8,128)(2,1)S(1)} %get-tuple-element.13.panel_ref.refs_0_), channel_id=1, source_target_pairs={{0,2},{1,3},{2,0},{3,1},{4,6},{5,7},{6,4},{7,5},{8,10},{9,11},{10,... | collective-permute-start | bytes 393224 | tf_op jit(solution)/shard_map/ppermute | solution.py:235
  6.6 4.6 %collective-permute-start.7 = (bf16[256,128]{1,0:T(8,128)(2,1)S(1)}, bf16[256,128]{1,0:T(8,128)(2,1)S(1)}, u32[]{:S(2)}, u32[]{:S(2)}) collective-permute-start(bf16[256,128]{1,0:T(8,128)(2,1)S(1)} %get-tuple-element.16), channel_id=1, source_target_pairs={{0,8},{8,0},{16,24},{24,16},{1,9},{9,1},{17,25},{25,17},{2,10},{10... | collective-permute-start | bytes 196616 | tf_op jit(solution)/shard_map/ppermute | solution.py:235
  8.6 7.2 %collective-permute-start.8 = (bf16[256,128]{1,0:T(8,128)(2,1)S(1)}, bf16[256,128]{1,0:T(8,128)(2,1)S(1)}, u32[]{:S(2)}, u32[]{:S(2)}) collective-permute-start(bf16[256,128]{1,0:T(8,128)(2,1)S(1)} %get-tuple-element.17), channel_id=1, source_target_pairs={{0,16},{8,24},{16,0},{24,8},{1,17},{9,25},{17,1},{25,9},{2,18},{10... | collective-permute-start | bytes 196616 | tf_op jit(solution)/shard_map/ppermute | solution.py:235
  11.2 6.2 %collective-permute-start.9 = (bf16[256,128]{1,0:T(8,128)(2,1)S(1)}, bf16[256,128]{1,0:T(8,128)(2,1)S(1)}, u32[]{:S(2)}, u32[]{:S(2)}) collective-permute-start(bf16[256,128]{1,0:T(8,128)(2,1)S(1)} %get-tuple-element.18), channel_id=1, source_target_pairs={{0,24},{8,16},{16,8},{24,0},{1,25},{9,17},{17,9},{25,1},{2,26},{10... | collective-permute-start | bytes 196616 | tf_op jit(solution)/shard_map/ppermute | solution.py:235
  15.8 4.2 %collective-permute-start = (bf16[512,128]{1,0:T(8,128)(2,1)S(1)}, bf16[512,128]{1,0:T(8,128)(2,1)S(1)}, u32[]{:S(2)}, u32[]{:S(2)}) collective-permute-start(bf16[512,128]{1,0:T(8,128)(2,1)S(1)} %get-tuple-element.13.panel_ref.refs_0_), channel_id=1, source_target_pairs={{0,1},{1,0},{2,3},{3,2},{4,5},{5,4},{6,7},{7,6},{8,9},{9,8},{10,11... | collective-permute-start | bytes 393224 | tf_op jit(solution)/shard_map/ppermute | solution.py:235
  15.8 4.2 %collective-permute-start.6 = (bf16[512,128]{1,0:T(8,128)(2,1)S(1)}, bf16[512,128]{1,0:T(8,128)(2,1)S(1)}, u32[]{:S(2)}, u32[]{:S(2)}) collective-permute-start(bf16[512,128]{1,0:T(8,128)(2,1)S(1)} %collective-permute-done.5.refs_6_), channel_id=1, source_target_pairs={{0,1},{1,0},{2,3},{3,2},{4,5},{5,4},{6,7},{7,6},{8,9},{9,8},{10,11... | collective-permute-start | bytes 393224 | tf_op jit(solution)/shard_map/ppermute | solution.py:235
  16.3 3.7 %collective-permute-start.4 = (bf16[512,128]{1,0:T(8,128)(2,1)S(1)}, bf16[512,128]{1,0:T(8,128)(2,1)S(1)}, u32[]{:S(2)}, u32[]{:S(2)}) collective-permute-start(bf16[512,128]{1,0:T(8,128)(2,1)S(1)} %collective-permute-done.3.refs_4_), channel_id=1, source_target_pairs={{0,1},{1,0},{2,3},{3,2},{4,5},{5,4},{6,7},{7,6},{8,9},{9,8},{10,11... | collective-permute-start | bytes 393224 | tf_op jit(solution)/shard_map/ppermute | solution.py:235
  16.4 3.6 %collective-permute-start.2 = (bf16[512,128]{1,0:T(8,128)(2,1)S(1)}, bf16[512,128]{1,0:T(8,128)(2,1)S(1)}, u32[]{:S(2)}, u32[]{:S(2)}) collective-permute-start(bf16[512,128]{1,0:T(8,128)(2,1)S(1)} %collective-permute-done.1.refs_2_), channel_id=1, source_target_pairs={{0,1},{1,0},{2,3},{3,2},{4,5},{5,4},{6,7},{7,6},{8,9},{9,8},{10,11... | collective-permute-start | bytes 393224 | tf_op jit(solution)/shard_map/ppermute | solution.py:235
  17.3 14.2 %collective-permute-start.17 = (bf16[256,512]{1,0:T(8,128)(2,1)S(1)}, bf16[256,512]{1,0:T(8,128)(2,1)S(1)}, u32[]{:S(2)}, u32[]{:S(2)}) collective-permute-start(bf16[256,512]{1,0:T(8,128)(2,1)S(1)} %get-tuple-element.21), channel_id=1, source_target_pairs={{0,16},{8,24},{16,0},{24,8},{1,17},{9,25},{17,1},{25,9},{2,18},{10... | collective-permute-start | bytes 786440 | tf_op jit(solution)/shard_map/ppermute | solution.py:235
  20.1 13.7 %copy-start = (bf16[512,1024]{1,0:T(8,128)(2,1)S(1)}, bf16[512,1024]{1,0:T(8,128)(2,1)}, u32[]{:S(2)}) copy-start(bf16[512,1024]{1,0:T(8,128)(2,1)} %bound_ref.7) | copy-start | bytes 3145732
  20.1 13.7 %copy-start.3 = (bf16[128,512]{1,0:T(8,128)(2,1)S(1)}, bf16[128,512]{1,0:T(8,128)(2,1)}, u32[]{:S(2)}) copy-start(bf16[128,512]{1,0:T(8,128)(2,1)} %w_ref.4) | copy-start | bytes 393220
  20.1 13.7 %copy-start.4 = (f32[512]{0:T(512)S(1)}, f32[512]{0:T(512)}, u32[]{:S(2)}) copy-start(f32[512]{0:T(512)} %param.21) | copy-start | bytes 6148
  21.5 10.0 %collective-permute-start.15 = (bf16[512,128]{1,0:T(8,128)(2,1)S(1)}, bf16[512,128]{1,0:T(8,128)(2,1)S(1)}, u32[]{:S(2)}, u32[]{:S(2)}) collective-permute-start(bf16[512,128]{1,0:T(8,128)(2,1)S(1)} %first.1.agg_ref.refs_0_), channel_id=1, source_target_pairs={{0,6},{1,7},{2,4},{3,5},{4,2},{5,3},{6,0},{7,1},{8,14},{9,15},{10,... | collective-permute-start | bytes 393224 | tf_op jit(solution)/shard_map/ppermute | solution.py:235
  24.0 9.2 %collective-permute-start.13 = (bf16[512,128]{1,0:T(8,128)(2,1)S(1)}, bf16[512,128]{1,0:T(8,128)(2,1)S(1)}, u32[]{:S(2)}, u32[]{:S(2)}) collective-permute-start(bf16[512,128]{1,0:T(8,128)(2,1)S(1)} %first.1.agg_ref.refs_0_), channel_id=1, source_target_pairs={{0,4},{1,5},{2,6},{3,7},{4,0},{5,1},{6,2},{7,3},{8,12},{9,13},{10,... | collective-permute-start | bytes 393224 | tf_op jit(solution)/shard_map/ppermute | solution.py:235
  24.5 8.7 %collective-permute-start.11 = (bf16[512,128]{1,0:T(8,128)(2,1)S(1)}, bf16[512,128]{1,0:T(8,128)(2,1)S(1)}, u32[]{:S(2)}, u32[]{:S(2)}) collective-permute-start(bf16[512,128]{1,0:T(8,128)(2,1)S(1)} %first.1.agg_ref.refs_0_), channel_id=1, source_target_pairs={{0,2},{1,3},{2,0},{3,1},{4,6},{5,7},{6,4},{7,5},{8,10},{9,11},{10,... | collective-permute-start | bytes 393224 | tf_op jit(solution)/shard_map/ppermute | solution.py:235
  25.0 8.6 %collective-permute-start.10 = (bf16[512,128]{1,0:T(8,128)(2,1)S(1)}, bf16[512,128]{1,0:T(8,128)(2,1)S(1)}, u32[]{:S(2)}, u32[]{:S(2)}) collective-permute-start(bf16[512,128]{1,0:T(8,128)(2,1)S(1)} %first.1.agg_ref.refs_0_), channel_id=1, source_target_pairs={{0,1},{1,0},{2,3},{3,2},{4,5},{5,4},{6,7},{7,6},{8,9},{9,8},{10,11... | collective-permute-start | bytes 393224 | tf_op jit(solution)/shard_map/ppermute | solution.py:235
  31.5 8.9 %collective-permute-start.18 = (bf16[256,512]{1,0:T(8,128)(2,1)S(1)}, bf16[256,512]{1,0:T(8,128)(2,1)S(1)}, u32[]{:S(2)}, u32[]{:S(2)}) collective-permute-start(bf16[256,512]{1,0:T(8,128)(2,1)S(1)} %get-tuple-element.22), channel_id=1, source_target_pairs={{0,8},{8,0},{16,24},{24,16},{1,9},{9,1},{17,25},{25,17},{2,10},{10... | collective-permute-start | bytes 786440 | tf_op jit(solution)/shard_map/ppermute | solution.py:235
  31.5 13.9 %collective-permute-start.19 = (bf16[256,512]{1,0:T(8,128)(2,1)S(1)}, bf16[256,512]{1,0:T(8,128)(2,1)S(1)}, u32[]{:S(2)}, u32[]{:S(2)}) collective-permute-start(bf16[256,512]{1,0:T(8,128)(2,1)S(1)} %get-tuple-element.23), channel_id=1, source_target_pairs={{0,24},{8,16},{16,8},{24,0},{1,25},{9,17},{17,9},{25,1},{2,26},{10... | collective-permute-start | bytes 786440 | tf_op jit(solution)/shard_map/ppermute | solution.py:235
  33.2 1.8 %collective-permute-start.16 = (bf16[512,128]{1,0:T(8,128)(2,1)S(1)}, bf16[512,128]{1,0:T(8,128)(2,1)S(1)}, u32[]{:S(2)}, u32[]{:S(2)}) collective-permute-start(bf16[512,128]{1,0:T(8,128)(2,1)S(1)} %collective-permute-done.15.refs_6_), channel_id=1, source_target_pairs={{0,1},{1,0},{2,3},{3,2},{4,5},{5,4},{6,7},{7,6},{8,9},{9,8},{10,11... | collective-permute-start | bytes 393224 | tf_op jit(solution)/shard_map/ppermute | solution.py:235
  33.2 1.8 %collective-permute-start.14 = (bf16[512,128]{1,0:T(8,128)(2,1)S(1)}, bf16[512,128]{1,0:T(8,128)(2,1)S(1)}, u32[]{:S(2)}, u32[]{:S(2)}) collective-permute-start(bf16[512,128]{1,0:T(8,128)(2,1)S(1)} %collective-permute-done.13.refs_4_), channel_id=1, source_target_pairs={{0,1},{1,0},{2,3},{3,2},{4,5},{5,4},{6,7},{7,6},{8,9},{9,8},{10,11... | collective-permute-start | bytes 393224 | tf_op jit(solution)/shard_map/ppermute | solution.py:235
  33.7 1.3 %collective-permute-start.12 = (bf16[512,128]{1,0:T(8,128)(2,1)S(1)}, bf16[512,128]{1,0:T(8,128)(2,1)S(1)}, u32[]{:S(2)}, u32[]{:S(2)}) collective-permute-start(bf16[512,128]{1,0:T(8,128)(2,1)S(1)} %collective-permute-done.11.refs_2_), channel_id=1, source_target_pairs={{0,1},{1,0},{2,3},{3,2},{4,5},{5,4},{6,7},{7,6},{8,9},{9,8},{10,11... | collective-permute-start | bytes 393224 | tf_op jit(solution)/shard_map/ppermute | solution.py:235
  35.0 10.3 %copy-start.2 = (bf16[512,512]{1,0:T(8,128)(2,1)S(1)}, bf16[512,512]{1,0:T(8,128)(2,1)}, u32[]{:S(2)}) copy-start(bf16[512,512]{1,0:T(8,128)(2,1)} %w_ref.5) | copy-start | bytes 1572868
  35.0 10.3 %copy-start.5 = (f32[512]{0:T(512)S(1)}, f32[512]{0:T(512)}, u32[]{:S(2)}) copy-start(f32[512]{0:T(512)} %param.23) | copy-start | bytes 6148
where the time goes:
time: 47.1 us; the launch traced here: 47 us
  starting transfers between devices  20.5 us (44%)
  waiting for transfers between devices  16.2 us (34%)
  Pallas kernels  9.48 us (20%)
  between operations  0.77 us (2%)
    ppermute x20, starting transfers between devices, swap(): lax.ppermute(block, axis, [(i, i ^ apart) for i in range(lax.axis_size(ax...  20.5 us
    ppermute x20, waiting for transfers between devices, swap(): lax.ppermute(block, axis, [(i, i ^ apart) for i in range(lax.axis_size(ax...  16.2 us
    pallas_call x1, Pallas kernels, others_part(): pl.pallas_call(functools.partial(others_kernel, len(panels), tuple(border...  2.1 us
    pallas_call x1, Pallas kernels, early_part(): pl.pallas_call(early_kernel, out_shape=[pltpu.VMEM((adj.shape[0], adj.sha...  1.87 us
    pallas_call x1, Pallas kernels, last_layer(): pl.pallas_call(functools.partial(last_kernel, tuple(border)), out_shape=j...  1.6 us
    pallas_call x1, Pallas kernels, first_layer(): pl.pallas_call(functools.partial(first_kernel, len(panels)), out_shape=pl...  1.39 us
    pallas_call x1, Pallas kernels, pack(): pl.pallas_call(pack_kernel, out_shape=[pltpu.VMEM(panels[0].shape, panels...  1.32 us
    pallas_call x1, Pallas kernels, own_part(): pl.pallas_call(functools.partial(own_kernel, tuple(border)), out_shape=[j...  1.2 us
  transfers between devices with their start and end apart: 20, of which 6 were waited for; matrix products, arithmetic and copies ran while one was open for 0% of the time, Pallas kernels for 14%

commit v1 on v0

--- a/solution.py
+++ b/solution.py
@@ -117,7 +117,7 @@
         out_shape=[pltpu.VMEM((adj.shape[0], adj.shape[1] * adj.shape[2]), BF16), pltpu.VMEM(panel.shape, F32)],
         in_specs=[pl.BlockSpec(memory_space=pltpu.HBM), VMEM],
         out_specs=[VMEM] * 2,
-        scratch_shapes=[pltpu.VMEM(adj.shape, BF16), pltpu.SemaphoreType.DMA((4,))],
+        scratch_shapes=[pltpu.VMEM(adj.shape, BF16), pltpu.SemaphoreType.DMA((8,))],
         compiler_params=pltpu.CompilerParams(vmem_limit_bytes=12 * MIB),
         name="early",
     )(far(adj), near(panel))
@@ -205,13 +205,13 @@
     border_refs = refs[:len(distances)]
     out_ref, held_ref, sems = refs[len(distances):]
     dom = lax.axis_index("dom")
+    total = (total_ref[...] + border_product(dom, bound_ref, border_refs, distances)).astype(BF16)
     chunks = sems.shape[0]
     rows = total_ref.shape[0] // chunks
     copies = []
     for n in range(chunks):
         here = pl.ds(n * rows, rows)
-        total = total_ref[here, :] + border_product(dom, bound_ref.at[here, :], border_refs, distances)
-        held_ref[here, :] = (dot(total.astype(BF16), w_ref[...]) + b_ref[...]).astype(BF16)
+        held_ref[here, :] = (dot(total[n * rows:(n + 1) * rows], w_ref[...]) + b_ref[...]).astype(BF16)
         copies.append(pltpu.make_async_copy(held_ref.at[here, :], out_ref.at[here, :], sems.at[n]))
         copies[n].start()
     for copy in copies:
@@ -225,7 +225,7 @@
         out_shape=jax.ShapeDtypeStruct(shape, BF16),
         in_specs=[VMEM] * (4 + len(border)),
         out_specs=pl.BlockSpec(memory_space=pltpu.HBM),
-        scratch_shapes=[pltpu.VMEM(shape, BF16), pltpu.SemaphoreType.DMA((2,))],
+        scratch_shapes=[pltpu.VMEM(shape, BF16), pltpu.SemaphoreType.DMA((4,))],
         compiler_params=pltpu.CompilerParams(vmem_limit_bytes=6 * MIB),
         name="last",
     )(*map(near, (total, bound, w_out, b_out, *border.values())))

time: 47.1 us -> 47 us (level)
  no operation moved by 1% of the time
where the time goes in v1:
time: 47 us; the launch traced here: 46.8 us
  starting transfers between devices  20.5 us (44%)
  waiting for transfers between devices  16.2 us (34%)
  Pallas kernels  9.31 us (20%)
  between operations  0.77 us (2%)
    ppermute x20, starting transfers between devices, swap(): lax.ppermute(block, axis, [(i, i ^ apart) for i in range(lax.axis_size(ax...  20.5 us
    ppermute x20, waiting for transfers between devices, swap(): lax.ppermute(block, axis, [(i, i ^ apart) for i in range(lax.axis_size(ax...  16.2 us
    pallas_call x1, Pallas kernels, others_part(): pl.pallas_call(functools.partial(others_kernel, len(panels), tuple(border...  2.1 us
    pallas_call x1, Pallas kernels, early_part(): pl.pallas_call(early_kernel, out_shape=[pltpu.VMEM((adj.shape[0], adj.sha...  1.88 us
    pallas_call x1, Pallas kernels, last_layer(): pl.pallas_call(functools.partial(last_kernel, tuple(border)), out_shape=j...  1.41 us
    pallas_call x1, Pallas kernels, first_layer(): pl.pallas_call(functools.partial(first_kernel, len(panels)), out_shape=pl...  1.39 us
    pallas_call x1, Pallas kernels, pack(): pl.pallas_call(pack_kernel, out_shape=[pltpu.VMEM(panels[0].shape, panels...  1.32 us
    pallas_call x1, Pallas kernels, own_part(): pl.pallas_call(functools.partial(own_kernel, tuple(border)), out_shape=[j...  1.2 us
  transfers between devices with their start and end apart: 20, of which 6 were waited for; matrix products, arithmetic and copies ran while one was open for 0% of the time, Pallas kernels for 14%

profile of v1, /device:TPU:0, one launch (start us, length us, event | category | flops | bytes accessed | tf_op | source)
XLA Modules:
  0.0 46.8 jit_solution(3983742946928162866)
XLA Ops:
  0.6 0.0 copy-start.6
  0.6 0.0 copy-start.1
  0.7 1.3 %pack.1 = (bf16[512,128]{1,0:T(8,128)(2,1)S(1)}, bf16[256,128]{1,0:T(8,128)(2,1)S(1)}, bf16[256,128]{1,0:T(8,128)(2,1)S(1)}, bf16[256,128]{1,0:T(8,128)(2,1)S(1)...) custom-call(s32[2,1,1,2,4]{4,3,2,1,0:T(2,128)} %bitcast.6, ...), custom_call_target="tpu_custom_call" | custom-call | tf_op jit(solution)/shard_map/pack/pallas_call | solution.py:65
  2.0 4.0 %collective-permute-start.5 = (bf16[512,128]{1,0:T(8,128)(2,1)S(1)}, bf16[512,128]{1,0:T(8,128)(2,1)S(1)}, u32[]{:S(2)}, u32[]{:S(2)}) collective-permute-start(bf16[512,128]{1,0:T(8,128)(2,1)S(1)} %get-tuple-element.13.panel_ref.refs_0_), channel_id=1, source_target_pairs={{0,6},{1,7},{2,4},{3,5},{4,2},{5,3},{6,0},{7,1},{8,14},{9,15},{10,... | collective-permute-start | bytes 393224 | tf_op jit(solution)/shard_map/ppermute | solution.py:235
  6.0 0.5 %collective-permute-start.3 = (bf16[512,128]{1,0:T(8,128)(2,1)S(1)}, bf16[512,128]{1,0:T(8,128)(2,1)S(1)}, u32[]{:S(2)}, u32[]{:S(2)}) collective-permute-start(bf16[512,128]{1,0:T(8,128)(2,1)S(1)} %get-tuple-element.13.panel_ref.refs_0_), channel_id=1, source_target_pairs={{0,4},{1,5},{2,6},{3,7},{4,0},{5,1},{6,2},{7,3},{8,12},{9,13},{10,... | collective-permute-start | bytes 393224 | tf_op jit(solution)/shard_map/ppermute | solution.py:235
  6.5 0.1 collective-permute-start.1
  6.6 2.0 %collective-permute-start.7 = (bf16[256,128]{1,0:T(8,128)(2,1)S(1)}, bf16[256,128]{1,0:T(8,128)(2,1)S(1)}, u32[]{:S(2)}, u32[]{:S(2)}) collective-permute-start(bf16[256,128]{1,0:T(8,128)(2,1)S(1)} %get-tuple-element.16), channel_id=1, source_target_pairs={{0,8},{8,0},{16,24},{24,16},{1,9},{9,1},{17,25},{25,17},{2,10},{10... | collective-permute-start | bytes 196616 | tf_op jit(solution)/shard_map/ppermute | solution.py:235
  8.6 2.6 %collective-permute-start.8 = (bf16[256,128]{1,0:T(8,128)(2,1)S(1)}, bf16[256,128]{1,0:T(8,128)(2,1)S(1)}, u32[]{:S(2)}, u32[]{:S(2)}) collective-permute-start(bf16[256,128]{1,0:T(8,128)(2,1)S(1)} %get-tuple-element.17), channel_id=1, source_target_pairs={{0,16},{8,24},{16,0},{24,8},{1,17},{9,25},{17,1},{25,9},{2,18},{10... | collective-permute-start | bytes 196616 | tf_op jit(solution)/shard_map/ppermute | solution.py:235
  11.2 0.0 collective-permute-done.7.refs_8_
  11.2 3.7 %collective-permute-start.9 = (bf16[256,128]{1,0:T(8,128)(2,1)S(1)}, bf16[256,128]{1,0:T(8,128)(2,1)S(1)}, u32[]{:S(2)}, u32[]{:S(2)}) collective-permute-start(bf16[256,128]{1,0:T(8,128)(2,1)S(1)} %get-tuple-element.18), channel_id=1, source_target_pairs={{0,24},{8,16},{16,8},{24,0},{1,25},{9,17},{17,9},{25,1},{2,26},{10... | collective-permute-start | bytes 196616 | tf_op jit(solution)/shard_map/ppermute | solution.py:235
  14.9 1.0 %collective-permute-done.8.refs_9_ = bf16[256,128]{1,0:T(8,128)(2,1)S(1)} collective-permute-done((bf16[256,128]{1,0:T(8,128)(2,1)S(1)}, bf16[256,128]{1,0:T(8,128)(2,1)S(1)}, u32[]{:S(2)}, u32[]{:S(2)}) %collective-permute-start.8) | collective-permute-done | bytes 65568 | tf_op jit(solution)/shard_map/ppermute | solution.py:235
  15.8 0.0 collective-permute-start
  15.8 0.0 collective-permute-done.5.refs_6_
  15.8 0.5 %collective-permute-start.6 = (bf16[512,128]{1,0:T(8,128)(2,1)S(1)}, bf16[512,128]{1,0:T(8,128)(2,1)S(1)}, u32[]{:S(2)}, u32[]{:S(2)}) collective-permute-start(bf16[512,128]{1,0:T(8,128)(2,1)S(1)} %collective-permute-done.5.refs_6_), channel_id=1, source_target_pairs={{0,1},{1,0},{2,3},{3,2},{4,5},{5,4},{6,7},{7,6},{8,9},{9,8},{10,11... | collective-permute-start | bytes 393224 | tf_op jit(solution)/shard_map/ppermute | solution.py:235
  16.3 0.0 collective-permute-done.3.refs_4_
  16.3 0.1 collective-permute-start.4
  16.4 0.0 collective-permute-done.1.refs_2_
  16.4 0.4 collective-permute-start.2
  16.9 0.5 %collective-permute-done.9.refs_10_ = bf16[256,128]{1,0:T(8,128)(2,1)S(1)} collective-permute-done((bf16[256,128]{1,0:T(8,128)(2,1)S(1)}, bf16[256,128]{1,0:T(8,128)(2,1)S(1)}, u32[]{:S(2)}, u32[]{:S(2)}) %collective-permute-start.9) | collective-permute-done | bytes 65568 | tf_op jit(solution)/shard_map/ppermute | solution.py:235
  17.3 0.8 %collective-permute-start.17 = (bf16[256,512]{1,0:T(8,128)(2,1)S(1)}, bf16[256,512]{1,0:T(8,128)(2,1)S(1)}, u32[]{:S(2)}, u32[]{:S(2)}) collective-permute-start(bf16[256,512]{1,0:T(8,128)(2,1)S(1)} %get-tuple-element.21), channel_id=1, source_target_pairs={{0,16},{8,24},{16,0},{24,8},{1,17},{9,25},{17,1},{25,9},{2,18},{10... | collective-permute-start | bytes 786440 | tf_op jit(solution)/shard_map/ppermute | solution.py:235
  18.1 1.9 %early.1 = (bf16[512,2048]{1,0:T(8,128)(2,1)S(1)}, f32[512,128]{1,0:T(8,128)S(1)}) custom-call(bf16[512,4,512]{2,1,0:T(4,128)(2,1)} %adj_ref.1, bf16[512,128]{1,0:T(8,128)(2,1)S(1)} %get-tuple-element.13.panel_ref.refs_0_), custom_call_target="tpu_custom_call" | custom-call | tf_op jit(solution)/shard_map/early/pallas_call | solution.py:115
  20.0 0.0 collective-permute-done.refs_1_
  20.0 0.0 collective-permute-done.6.refs_7_
  20.0 0.0 collective-permute-done.4.refs_5_
  20.0 0.0 collective-permute-done.2.refs_3_
  20.1 0.0 copy-done.6
  20.1 0.0 copy-done.1
  20.1 0.0 copy-start
  20.1 0.0 copy-start.3
  20.1 0.0 copy-start.4
  20.1 1.4 %first.1.agg_ref.refs_0_ = bf16[512,128]{1,0:T(8,128)(2,1)S(1)} custom-call(s32[1,1,4]{2,1,0:T(1,128)S(1)} %copy-done.6, bf16[512,2048]{1,0:T(8,128)(2,1)S(1)} %get-tuple-element.14.tiles_ref, f32[512,128]{1,0:T(8,128)S(1)} %get-tuple-element.15.total_ref, bf16[512,1024]{1,0:T(8,128)(2,1)S(1)} %copy-done.1, ...), custom_call_target="tpu_custom_call" | custom-call | tf_op jit(solution)/shard_map/first/pallas_call | solution.py:138
  21.5 2.5 %collective-permute-start.15 = (bf16[512,128]{1,0:T(8,128)(2,1)S(1)}, bf16[512,128]{1,0:T(8,128)(2,1)S(1)}, u32[]{:S(2)}, u32[]{:S(2)}) collective-permute-start(bf16[512,128]{1,0:T(8,128)(2,1)S(1)} %first.1.agg_ref.refs_0_), channel_id=1, source_target_pairs={{0,6},{1,7},{2,4},{3,5},{4,2},{5,3},{6,0},{7,1},{8,14},{9,15},{10,... | collective-permute-start | bytes 393224 | tf_op jit(solution)/shard_map/ppermute | solution.py:235
  24.0 0.5 %collective-permute-start.13 = (bf16[512,128]{1,0:T(8,128)(2,1)S(1)}, bf16[512,128]{1,0:T(8,128)(2,1)S(1)}, u32[]{:S(2)}, u32[]{:S(2)}) collective-permute-start(bf16[512,128]{1,0:T(8,128)(2,1)S(1)} %first.1.agg_ref.refs_0_), channel_id=1, source_target_pairs={{0,4},{1,5},{2,6},{3,7},{4,0},{5,1},{6,2},{7,3},{8,12},{9,13},{10,... | collective-permute-start | bytes 393224 | tf_op jit(solution)/shard_map/ppermute | solution.py:235
  24.5 0.5 %collective-permute-start.11 = (bf16[512,128]{1,0:T(8,128)(2,1)S(1)}, bf16[512,128]{1,0:T(8,128)(2,1)S(1)}, u32[]{:S(2)}, u32[]{:S(2)}) collective-permute-start(bf16[512,128]{1,0:T(8,128)(2,1)S(1)} %first.1.agg_ref.refs_0_), channel_id=1, source_target_pairs={{0,2},{1,3},{2,0},{3,1},{4,6},{5,7},{6,4},{7,5},{8,10},{9,11},{10,... | collective-permute-start | bytes 393224 | tf_op jit(solution)/shard_map/ppermute | solution.py:235
  25.1 0.0 collective-permute-start.10
  25.1 6.4 %collective-permute-done.17.refs_8_ = bf16[256,512]{1,0:T(8,128)(2,1)S(1)} collective-permute-done((bf16[256,512]{1,0:T(8,128)(2,1)S(1)}, bf16[256,512]{1,0:T(8,128)(2,1)S(1)}, u32[]{:S(2)}, u32[]{:S(2)}) %collective-permute-start.17) | collective-permute-done | bytes 262176 | tf_op jit(solution)/shard_map/ppermute | solution.py:235
  31.5 0.0 collective-permute-start.18
  31.5 0.0 collective-permute-done.15.refs_6_
  31.5 1.7 %collective-permute-start.19 = (bf16[256,512]{1,0:T(8,128)(2,1)S(1)}, bf16[256,512]{1,0:T(8,128)(2,1)S(1)}, u32[]{:S(2)}, u32[]{:S(2)}) collective-permute-start(bf16[256,512]{1,0:T(8,128)(2,1)S(1)} %get-tuple-element.23), channel_id=1, source_target_pairs={{0,24},{8,16},{16,8},{24,0},{1,25},{9,17},{17,9},{25,1},{2,26},{10... | collective-permute-start | bytes 786440 | tf_op jit(solution)/shard_map/ppermute | solution.py:235
  33.2 0.0 collective-permute-done.13.refs_4_
  33.2 0.0 collective-permute-start.16
  33.2 0.0 collective-permute-done.11.refs_2_
  33.2 0.5 %collective-permute-start.14 = (bf16[512,128]{1,0:T(8,128)(2,1)S(1)}, bf16[512,128]{1,0:T(8,128)(2,1)S(1)}, u32[]{:S(2)}, u32[]{:S(2)}) collective-permute-start(bf16[512,128]{1,0:T(8,128)(2,1)S(1)} %collective-permute-done.13.refs_4_), channel_id=1, source_target_pairs={{0,1},{1,0},{2,3},{3,2},{4,5},{5,4},{6,7},{7,6},{8,9},{9,8},{10,11... | collective-permute-start | bytes 393224 | tf_op jit(solution)/shard_map/ppermute | solution.py:235
  33.7 0.0 collective-permute-done.10.refs_1_
  33.7 0.1 collective-permute-start.12
  33.8 0.0 copy-done
  33.8 0.0 copy-done.3
  33.8 0.0 copy-done.4
  33.8 1.2 %own.1 = (bf16[512,512]{1,0:T(8,128)(2,1)}, f32[512,512]{1,0:T(8,128)S(1)}) custom-call(bf16[512,2048]{1,0:T(8,128)(2,1)S(1)} %get-tuple-element.14.tiles_ref, bf16[128,512]{1,0:T(8,128)(2,1)S(1)} %copy-done.3, f32[1,512]{1,0:T(1,128)S(1)} %bitcast.3, bf16[512,128]{1,0:T(8,128)(2,1)S(1)} %first.1.agg_ref.refs_0_, bf16[512,1024]{1,0:T(8,128)(2,1)S(1)} %copy-done), custom_call_target="tpu_custom_call" | custom-call | tf_op jit(solution)/shard_map/own/pallas_call | solution.py:165
  35.0 0.0 collective-permute-done.16.refs_7_
  35.0 0.0 collective-permute-done.14.refs_5_
  35.0 0.1 collective-permute-done.12.refs_3_
  35.0 0.0 copy-start.2
  35.0 0.0 copy-start.5
  35.0 2.1 %others.1.total_ref = f32[512,512]{1,0:T(8,128)S(1)} custom-call(s32[1,1,4]{2,1,0:T(1,128)S(1)} %copy-done.6, bf16[512,2048]{1,0:T(8,128)(2,1)S(1)} %get-tuple-element.14.tiles_ref, bf16[128,512]{1,0:T(8,128)(2,1)S(1)} %copy-done.3, f32[1,512]{1,0:T(1,128)S(1)} %bitcast.4, f32[512,512]{1,0:T(8,128)S(1)} %get-tuple-element.20.total_ref, ...), custom_call_target="tpu_custom_call" | custom-call | tf_op jit(solution)/shard_map/others/pallas_call | solution.py:190
  37.2 3.2 %collective-permute-done.18.refs_0_ = bf16[256,512]{1,0:T(8,128)(2,1)S(1)} collective-permute-done((bf16[256,512]{1,0:T(8,128)(2,1)S(1)}, bf16[256,512]{1,0:T(8,128)(2,1)S(1)}, u32[]{:S(2)}, u32[]{:S(2)}) %collective-permute-start.18) | collective-permute-done | bytes 262176 | tf_op jit(solution)/shard_map/ppermute | solution.py:235
  40.4 5.0 %collective-permute-done.19.refs_1_ = bf16[256,512]{1,0:T(8,128)(2,1)S(1)} collective-permute-done((bf16[256,512]{1,0:T(8,128)(2,1)S(1)}, bf16[256,512]{1,0:T(8,128)(2,1)S(1)}, u32[]{:S(2)}, u32[]{:S(2)}) %collective-permute-start.19) | collective-permute-done | bytes 262176 | tf_op jit(solution)/shard_map/ppermute | solution.py:235
  45.4 0.0 copy-done.2
  45.4 0.0 copy-done.5
  45.4 1.4 %last.1 = bf16[512,512]{1,0:T(8,128)(2,1)} custom-call(f32[512,512]{1,0:T(8,128)S(1)} %others.1.total_ref, bf16[512,1024]{1,0:T(8,128)(2,1)S(1)} %copy-done, bf16[512,512]{1,0:T(8,128)(2,1)S(1)} %copy-done.2, f32[1,512]{1,0:T(1,128)S(1)} %bitcast.5, bf16[256,512]{1,0:T(8,128)(2,1)S(1)} %collective-permute-done.18.refs_0_, ...), custom_call_target="tpu_custom_call" | custom-call | tf_op jit(solution)/shard_map/last/pallas_call | solution.py:223
Async XLA Ops:
  0.6 19.4 %copy-start.6 = (s32[1,1,4]{2,1,0:T(1,128)S(1)}, s32[1,1,4]{2,1,0:T(1,128)}, u32[]{:S(2)}) copy-start(s32[1,1,4]{2,1,0:T(1,128)} %cols_ref.3) | copy-start | bytes 52
  0.6 19.4 %copy-start.1 = (bf16[512,1024]{1,0:T(8,128)(2,1)S(1)}, bf16[512,1024]{1,0:T(8,128)(2,1)}, u32[]{:S(2)}) copy-start(bf16[512,1024]{1,0:T(8,128)(2,1)} %bound_ref.4) | copy-start | bytes 3145732
  2.0 13.8 %collective-permute-start.5 = (bf16[512,128]{1,0:T(8,128)(2,1)S(1)}, bf16[512,128]{1,0:T(8,128)(2,1)S(1)}, u32[]{:S(2)}, u32[]{:S(2)}) collective-permute-start(bf16[512,128]{1,0:T(8,128)(2,1)S(1)} %get-tuple-element.13.panel_ref.refs_0_), channel_id=1, source_target_pairs={{0,6},{1,7},{2,4},{3,5},{4,2},{5,3},{6,0},{7,1},{8,14},{9,15},{10,... | collective-permute-start | bytes 393224 | tf_op jit(solution)/shard_map/ppermute | solution.py:235
  6.0 10.4 %collective-permute-start.3 = (bf16[512,128]{1,0:T(8,128)(2,1)S(1)}, bf16[512,128]{1,0:T(8,128)(2,1)S(1)}, u32[]{:S(2)}, u32[]{:S(2)}) collective-permute-start(bf16[512,128]{1,0:T(8,128)(2,1)S(1)} %get-tuple-element.13.panel_ref.refs_0_), channel_id=1, source_target_pairs={{0,4},{1,5},{2,6},{3,7},{4,0},{5,1},{6,2},{7,3},{8,12},{9,13},{10,... | collective-permute-start | bytes 393224 | tf_op jit(solution)/shard_map/ppermute | solution.py:235
  6.5 9.9 %collective-permute-start.1 = (bf16[512,128]{1,0:T(8,128)(2,1)S(1)}, bf16[512,128]{1,0:T(8,128)(2,1)S(1)}, u32[]{:S(2)}, u32[]{:S(2)}) collective-permute-start(bf16[512,128]{1,0:T(8,128)(2,1)S(1)} %get-tuple-element.13.panel_ref.refs_0_), channel_id=1, source_target_pairs={{0,2},{1,3},{2,0},{3,1},{4,6},{5,7},{6,4},{7,5},{8,10},{9,11},{10,... | collective-permute-start | bytes 393224 | tf_op jit(solution)/shard_map/ppermute | solution.py:235
  6.6 4.6 %collective-permute-start.7 = (bf16[256,128]{1,0:T(8,128)(2,1)S(1)}, bf16[256,128]{1,0:T(8,128)(2,1)S(1)}, u32[]{:S(2)}, u32[]{:S(2)}) collective-permute-start(bf16[256,128]{1,0:T(8,128)(2,1)S(1)} %get-tuple-element.16), channel_id=1, source_target_pairs={{0,8},{8,0},{16,24},{24,16},{1,9},{9,1},{17,25},{25,17},{2,10},{10... | collective-permute-start | bytes 196616 | tf_op jit(solution)/shard_map/ppermute | solution.py:235
  8.6 7.2 %collective-permute-start.8 = (bf16[256,128]{1,0:T(8,128)(2,1)S(1)}, bf16[256,128]{1,0:T(8,128)(2,1)S(1)}, u32[]{:S(2)}, u32[]{:S(2)}) collective-permute-start(bf16[256,128]{1,0:T(8,128)(2,1)S(1)} %get-tuple-element.17), channel_id=1, source_target_pairs={{0,16},{8,24},{16,0},{24,8},{1,17},{9,25},{17,1},{25,9},{2,18},{10... | collective-permute-start | bytes 196616 | tf_op jit(solution)/shard_map/ppermute | solution.py:235
  11.2 6.2 %collective-permute-start.9 = (bf16[256,128]{1,0:T(8,128)(2,1)S(1)}, bf16[256,128]{1,0:T(8,128)(2,1)S(1)}, u32[]{:S(2)}, u32[]{:S(2)}) collective-permute-start(bf16[256,128]{1,0:T(8,128)(2,1)S(1)} %get-tuple-element.18), channel_id=1, source_target_pairs={{0,24},{8,16},{16,8},{24,0},{1,25},{9,17},{17,9},{25,1},{2,26},{10... | collective-permute-start | bytes 196616 | tf_op jit(solution)/shard_map/ppermute | solution.py:235
  15.8 4.2 %collective-permute-start = (bf16[512,128]{1,0:T(8,128)(2,1)S(1)}, bf16[512,128]{1,0:T(8,128)(2,1)S(1)}, u32[]{:S(2)}, u32[]{:S(2)}) collective-permute-start(bf16[512,128]{1,0:T(8,128)(2,1)S(1)} %get-tuple-element.13.panel_ref.refs_0_), channel_id=1, source_target_pairs={{0,1},{1,0},{2,3},{3,2},{4,5},{5,4},{6,7},{7,6},{8,9},{9,8},{10,11... | collective-permute-start | bytes 393224 | tf_op jit(solution)/shard_map/ppermute | solution.py:235
  15.8 4.2 %collective-permute-start.6 = (bf16[512,128]{1,0:T(8,128)(2,1)S(1)}, bf16[512,128]{1,0:T(8,128)(2,1)S(1)}, u32[]{:S(2)}, u32[]{:S(2)}) collective-permute-start(bf16[512,128]{1,0:T(8,128)(2,1)S(1)} %collective-permute-done.5.refs_6_), channel_id=1, source_target_pairs={{0,1},{1,0},{2,3},{3,2},{4,5},{5,4},{6,7},{7,6},{8,9},{9,8},{10,11... | collective-permute-start | bytes 393224 | tf_op jit(solution)/shard_map/ppermute | solution.py:235
  16.3 3.7 %collective-permute-start.4 = (bf16[512,128]{1,0:T(8,128)(2,1)S(1)}, bf16[512,128]{1,0:T(8,128)(2,1)S(1)}, u32[]{:S(2)}, u32[]{:S(2)}) collective-permute-start(bf16[512,128]{1,0:T(8,128)(2,1)S(1)} %collective-permute-done.3.refs_4_), channel_id=1, source_target_pairs={{0,1},{1,0},{2,3},{3,2},{4,5},{5,4},{6,7},{7,6},{8,9},{9,8},{10,11... | collective-permute-start | bytes 393224 | tf_op jit(solution)/shard_map/ppermute | solution.py:235
  16.4 3.6 %collective-permute-start.2 = (bf16[512,128]{1,0:T(8,128)(2,1)S(1)}, bf16[512,128]{1,0:T(8,128)(2,1)S(1)}, u32[]{:S(2)}, u32[]{:S(2)}) collective-permute-start(bf16[512,128]{1,0:T(8,128)(2,1)S(1)} %collective-permute-done.1.refs_2_), channel_id=1, source_target_pairs={{0,1},{1,0},{2,3},{3,2},{4,5},{5,4},{6,7},{7,6},{8,9},{9,8},{10,11... | collective-permute-start | bytes 393224 | tf_op jit(solution)/shard_map/ppermute | solution.py:235
  17.3 14.2 %collective-permute-start.17 = (bf16[256,512]{1,0:T(8,128)(2,1)S(1)}, bf16[256,512]{1,0:T(8,128)(2,1)S(1)}, u32[]{:S(2)}, u32[]{:S(2)}) collective-permute-start(bf16[256,512]{1,0:T(8,128)(2,1)S(1)} %get-tuple-element.21), channel_id=1, source_target_pairs={{0,16},{8,24},{16,0},{24,8},{1,17},{9,25},{17,1},{25,9},{2,18},{10... | collective-permute-start | bytes 786440 | tf_op jit(solution)/shard_map/ppermute | solution.py:235
  20.1 13.7 %copy-start = (bf16[512,1024]{1,0:T(8,128)(2,1)S(1)}, bf16[512,1024]{1,0:T(8,128)(2,1)}, u32[]{:S(2)}) copy-start(bf16[512,1024]{1,0:T(8,128)(2,1)} %bound_ref.7) | copy-start | bytes 3145732
  20.1 13.7 %copy-start.3 = (bf16[128,512]{1,0:T(8,128)(2,1)S(1)}, bf16[128,512]{1,0:T(8,128)(2,1)}, u32[]{:S(2)}) copy-start(bf16[128,512]{1,0:T(8,128)(2,1)} %w_ref.4) | copy-start | bytes 393220
  20.1 13.7 %copy-start.4 = (f32[512]{0:T(512)S(1)}, f32[512]{0:T(512)}, u32[]{:S(2)}) copy-start(f32[512]{0:T(512)} %param.21) | copy-start | bytes 6148
  21.5 10.0 %collective-permute-start.15 = (bf16[512,128]{1,0:T(8,128)(2,1)S(1)}, bf16[512,128]{1,0:T(8,128)(2,1)S(1)}, u32[]{:S(2)}, u32[]{:S(2)}) collective-permute-start(bf16[512,128]{1,0:T(8,128)(2,1)S(1)} %first.1.agg_ref.refs_0_), channel_id=1, source_target_pairs={{0,6},{1,7},{2,4},{3,5},{4,2},{5,3},{6,0},{7,1},{8,14},{9,15},{10,... | collective-permute-start | bytes 393224 | tf_op jit(solution)/shard_map/ppermute | solution.py:235
  24.0 9.2 %collective-permute-start.13 = (bf16[512,128]{1,0:T(8,128)(2,1)S(1)}, bf16[512,128]{1,0:T(8,128)(2,1)S(1)}, u32[]{:S(2)}, u32[]{:S(2)}) collective-permute-start(bf16[512,128]{1,0:T(8,128)(2,1)S(1)} %first.1.agg_ref.refs_0_), channel_id=1, source_target_pairs={{0,4},{1,5},{2,6},{3,7},{4,0},{5,1},{6,2},{7,3},{8,12},{9,13},{10,... | collective-permute-start | bytes 393224 | tf_op jit(solution)/shard_map/ppermute | solution.py:235
  24.5 8.7 %collective-permute-start.11 = (bf16[512,128]{1,0:T(8,128)(2,1)S(1)}, bf16[512,128]{1,0:T(8,128)(2,1)S(1)}, u32[]{:S(2)}, u32[]{:S(2)}) collective-permute-start(bf16[512,128]{1,0:T(8,128)(2,1)S(1)} %first.1.agg_ref.refs_0_), channel_id=1, source_target_pairs={{0,2},{1,3},{2,0},{3,1},{4,6},{5,7},{6,4},{7,5},{8,10},{9,11},{10,... | collective-permute-start | bytes 393224 | tf_op jit(solution)/shard_map/ppermute | solution.py:235
  25.1 8.6 %collective-permute-start.10 = (bf16[512,128]{1,0:T(8,128)(2,1)S(1)}, bf16[512,128]{1,0:T(8,128)(2,1)S(1)}, u32[]{:S(2)}, u32[]{:S(2)}) collective-permute-start(bf16[512,128]{1,0:T(8,128)(2,1)S(1)} %first.1.agg_ref.refs_0_), channel_id=1, source_target_pairs={{0,1},{1,0},{2,3},{3,2},{4,5},{5,4},{6,7},{7,6},{8,9},{9,8},{10,11... | collective-permute-start | bytes 393224 | tf_op jit(solution)/shard_map/ppermute | solution.py:235
  31.5 8.9 %collective-permute-start.18 = (bf16[256,512]{1,0:T(8,128)(2,1)S(1)}, bf16[256,512]{1,0:T(8,128)(2,1)S(1)}, u32[]{:S(2)}, u32[]{:S(2)}) collective-permute-start(bf16[256,512]{1,0:T(8,128)(2,1)S(1)} %get-tuple-element.22), channel_id=1, source_target_pairs={{0,8},{8,0},{16,24},{24,16},{1,9},{9,1},{17,25},{25,17},{2,10},{10... | collective-permute-start | bytes 786440 | tf_op jit(solution)/shard_map/ppermute | solution.py:235
  31.5 13.9 %collective-permute-start.19 = (bf16[256,512]{1,0:T(8,128)(2,1)S(1)}, bf16[256,512]{1,0:T(8,128)(2,1)S(1)}, u32[]{:S(2)}, u32[]{:S(2)}) collective-permute-start(bf16[256,512]{1,0:T(8,128)(2,1)S(1)} %get-tuple-element.23), channel_id=1, source_target_pairs={{0,24},{8,16},{16,8},{24,0},{1,25},{9,17},{17,9},{25,1},{2,26},{10... | collective-permute-start | bytes 786440 | tf_op jit(solution)/shard_map/ppermute | solution.py:235
  33.2 1.8 %collective-permute-start.16 = (bf16[512,128]{1,0:T(8,128)(2,1)S(1)}, bf16[512,128]{1,0:T(8,128)(2,1)S(1)}, u32[]{:S(2)}, u32[]{:S(2)}) collective-permute-start(bf16[512,128]{1,0:T(8,128)(2,1)S(1)} %collective-permute-done.15.refs_6_), channel_id=1, source_target_pairs={{0,1},{1,0},{2,3},{3,2},{4,5},{5,4},{6,7},{7,6},{8,9},{9,8},{10,11... | collective-permute-start | bytes 393224 | tf_op jit(solution)/shard_map/ppermute | solution.py:235
  33.2 1.8 %collective-permute-start.14 = (bf16[512,128]{1,0:T(8,128)(2,1)S(1)}, bf16[512,128]{1,0:T(8,128)(2,1)S(1)}, u32[]{:S(2)}, u32[]{:S(2)}) collective-permute-start(bf16[512,128]{1,0:T(8,128)(2,1)S(1)} %collective-permute-done.13.refs_4_), channel_id=1, source_target_pairs={{0,1},{1,0},{2,3},{3,2},{4,5},{5,4},{6,7},{7,6},{8,9},{9,8},{10,11... | collective-permute-start | bytes 393224 | tf_op jit(solution)/shard_map/ppermute | solution.py:235
  33.7 1.3 %collective-permute-start.12 = (bf16[512,128]{1,0:T(8,128)(2,1)S(1)}, bf16[512,128]{1,0:T(8,128)(2,1)S(1)}, u32[]{:S(2)}, u32[]{:S(2)}) collective-permute-start(bf16[512,128]{1,0:T(8,128)(2,1)S(1)} %collective-permute-done.11.refs_2_), channel_id=1, source_target_pairs={{0,1},{1,0},{2,3},{3,2},{4,5},{5,4},{6,7},{7,6},{8,9},{9,8},{10,11... | collective-permute-start | bytes 393224 | tf_op jit(solution)/shard_map/ppermute | solution.py:235
  35.0 10.3 %copy-start.2 = (bf16[512,512]{1,0:T(8,128)(2,1)S(1)}, bf16[512,512]{1,0:T(8,128)(2,1)}, u32[]{:S(2)}) copy-start(bf16[512,512]{1,0:T(8,128)(2,1)} %w_ref.5) | copy-start | bytes 1572868
  35.0 10.3 %copy-start.5 = (f32[512]{0:T(512)S(1)}, f32[512]{0:T(512)}, u32[]{:S(2)}) copy-start(f32[512]{0:T(512)} %param.23) | copy-start | bytes 6148
